TPU v7x, 128 devices: a whole 4x4x4 slice. The times are simulated.
128 devices in a mesh: tiles: 64 (over y, z_hi, x, core), vec: 2 (over z_lo).
Axes of the slice: x: 4, y: 4, z: 4 (z_hi: 2, z_lo: 2; z = z_hi * 2 + z_lo), core: 2. Of those that a mesh axis runs over, the one named last changes fastest.
Arguments:
- omega: float32 [128, 4, 512, 128], P('vec', None, 'tiles'), may hold values from -24 to 24
- conductance: float32 [3, 4, 512, 128], P(None, None, 'tiles'), may hold values from 0.02 to 0.16
- wet: int32 [512, 128], P('tiles'), may hold values 0 or 1
- volume: float32 [512, 128], P('tiles'), may hold values from 0.3 to 27, as said below
- face_runs: int32 [64, 4], P('tiles'), may hold values from 0 to 128, as said below
Outputs:
- diffused: float32 [128, 4, 512, 128], P('vec', None, 'tiles')
- r_factor: float32 [128, 128], replicated
Inputs may be any that keep to these rules, and one draw needn't show every extreme that they name: `face_runs`: tiles in tile row 0 have a closed lower row face and tiles in tile column 0 a closed lower column face (length 0); every other run lies within its face, covers at least half of it, and some tiles have fully open faces. Positive cell volume weights.
All inputs are finite; a program needn't handle non-finite values. No bound on the sum of `wet` on one device may be relied on, other than what follows from the above.
Results may differ from a plain program's by a relative error of at most 0.00005.
Values sent between devices are 32-bit elements; how exact they have to be, the bound alone decides.
A program may use at most 64 MiB of HBM per device.

v0:
```python
import jax
import jax.numpy as jnp
from jax import lax
from jax.sharding import PartitionSpec as P

TGY = 8
ITERS = 4


def shifted(value, axis, steps):
    count = lax.axis_size(axis)
    first, last = (max(0, -steps), min(count, count - steps))
    return lax.ppermute(value, axis, [(source, source + steps) for source in range(first, last)])


def diffuse(field, statics):
    cond_x = statics[0]
    cond_y = statics[1]
    cond_z = statics[2]
    wet_cells = statics[3]
    flux_x = cond_x[:, 1:, :] * (field[:, :, 1:, :] - field[:, :, :-1, :])
    flux_y = cond_y[:, :, 1:] * (field[:, :, :, 1:] - field[:, :, :, :-1])
    flux_z = cond_z[1:] * (field[:, 1:] - field[:, :-1])
    zero_level = jnp.zeros_like(field[:, :1])
    flux_z = jnp.concatenate([zero_level, flux_z, zero_level], axis=1)
    change = flux_x[:, :, 1:, 1:-1] - flux_x[:, :, :-1, 1:-1]
    change = change + flux_y[:, :, 1:-1, 1:] - flux_y[:, :, 1:-1, :-1]
    change = change + (flux_z[:, 1:] - flux_z[:, :-1])[:, :, 1:-1, 1:-1]
    return wet_cells[:, 1:-1, 1:-1] * (field[:, :, 1:-1, 1:-1] + change)


def moving(values, offset):
    return shifted(values, "tiles", offset)


def fixed_rim(values, offset):
    return shifted(values, "tiles", offset)


def extend(values, margin, neighbour):
    lower_rim = neighbour(values[:, :, -margin:, :], TGY)
    upper_rim = neighbour(values[:, :, :margin, :], -TGY)
    stacked = jnp.concatenate([lower_rim, values, upper_rim], axis=2)
    left_rim = neighbour(stacked[:, :, :, -margin:], 1)
    right_rim = neighbour(stacked[:, :, :, :margin], -1)
    return jnp.concatenate([left_rim, stacked, right_rim], axis=3)


def shards(omega, conductance, wet, volume, face_runs):
    levels = omega.shape[1]
    tile_rows = omega.shape[2]
    tile_cols = omega.shape[3]
    row_ids = lax.broadcasted_iota(jnp.int32, (tile_rows, tile_cols), 0)
    col_ids = lax.broadcasted_iota(jnp.int32, (tile_rows, tile_cols), 1)
    runs = face_runs[0]
    open_x = (col_ids >= runs[0]) & (col_ids < runs[0] + runs[1])
    factor_x = jnp.where(row_ids == 0, open_x.astype(jnp.float32), jnp.float32(1.0))
    open_y = (row_ids >= runs[2]) & (row_ids < runs[2] + runs[3])
    factor_y = jnp.where(col_ids == 0, open_y.astype(jnp.float32), jnp.float32(1.0))
    level_ids = lax.broadcasted_iota(jnp.int32, (levels, 1, 1), 0)
    cond_z = conductance[2] * (level_ids > 0).astype(jnp.float32)
    wet_float = wet.astype(jnp.float32)
    statics = jnp.stack(
        [
            conductance[0] * factor_x[None],
            conductance[1] * factor_y[None],
            cond_z,
            jnp.broadcast_to(wet_float[None], (levels, tile_rows, tile_cols)),
        ]
    )
    margin = 1
    statics_wide = extend(statics, margin, fixed_rim)
    field = wet_float[None, None] * omega
    for block_index in range(ITERS // margin):
        grown = extend(field, margin, moving)
        current = statics_wide
        grown = diffuse(grown, current)
        current = current[:, :, 1:-1, 1:-1]
        field = grown
    regrouped = lax.all_to_all(field, "vec", split_axis=1, concat_axis=0, tiled=True)
    all_vectors = regrouped.shape[0]
    total_cells = levels * lax.axis_size("tiles") * tile_rows * tile_cols
    flat_values = regrouped.reshape(all_vectors, -1)
    weighted = (regrouped * volume[None, None]).reshape(all_vectors, -1)
    gram_local = (
        lax.dot_general(
            weighted,
            flat_values,
            (((1,), (1,)), ((), ())),
            precision=lax.Precision.HIGHEST,
            preferred_element_type=jnp.float32,
        )
        / total_cells
    )
    gram = lax.psum(gram_local, ("tiles", "vec"))
    r_factor = jnp.linalg.cholesky(gram).T
    return (field, r_factor)


def solution(mesh):
    in_specs = (
        P("vec", None, "tiles", None),
        P(None, None, "tiles", None),
        P("tiles", None),
        P("tiles", None),
        P("tiles", None),
    )
    out_specs = (P("vec", None, "tiles", None), P())
    return jax.shard_map(shards, mesh=mesh, in_specs=in_specs, out_specs=out_specs, check_vma=False)
```

profile of v0, /device:TPU:1, one launch (start us, length us, event | category | flops | bytes accessed | tf_op | source)
XLA Modules:
  0.0 363.9 jit_solution(15413979670254158427)
XLA Ops:
  7.2 1.5 fusion.34
  13.2 0.8 slice_multiply_fusion.2
  14.1 6.3 %collective-permute-start = (f32[4,4,1,128]{3,2,1,0:T(1,128)S(1)}, f32[4,4,1,128]{3,2,1,0:T(1,128)S(1)}, u32[]{:S(2)}, u32[]{:S(2)}) collective-permute-start(f32[4,4,1,128]{3,2,1,0:T(1,128)S(1)} %get-tuple-element.29), channel_id=1, source_target_pairs={{0,16},{2,18},{4,20},{6,22},{8,24},{10,26},{12,28},{14,30},{16,32}... | collective-permute-start | bytes 24584 | tf_op jit(solution)/shard_map/ppermute | solution.py:13
  20.4 1.3 collective-permute-start.1
  21.7 1.8 copy_multiply_fusion
  23.6 2.7 collective-permute-done.1
  26.4 5.1 %collective-permute-start.2 = (f32[4,4,10,1]{3,2,1,0:T(8,128)S(1)}, f32[4,4,10,1]{3,2,1,0:T(8,128)S(1)}, u32[]{:S(2)}, u32[]{:S(2)}) collective-permute-start(f32[4,4,10,1]{3,2,1,0:T(8,128)S(1)} %get-tuple-element.27), channel_id=1, source_target_pairs={{0,2},{2,4},{4,6},{6,8},{8,10},{10,12},{12,14},{14,16},{16,18},{18... | collective-permute-start | bytes 1928 | tf_op jit(solution)/shard_map/ppermute | solution.py:13
  31.6 1.9 collective-permute-start.3
  33.5 3.2 collective-permute-start.4
  36.7 1.3 collective-permute-start.5
  38.6 5.3 %collective-permute-done.5 = f32[64,4,1,128]{3,0,2,1:T(8,128)S(1)} collective-permute-done((f32[64,4,1,128]{3,0,2,1:T(8,128)S(1)}, f32[64,4,1,128]{3,0,2,1:T(8,128)S(1)}, u32[]{:S(2)}, u32[]{:S(2)}) %collective-permute-start.5) | collective-permute-done | bytes 131104 | tf_op jit(solution)/shard_map/ppermute | solution.py:13
  44.0 1.5 fusion.28
  45.6 2.0 copy.15
  48.3 8.0 %collective-permute-start.7 = (f32[64,4,10,1]{0,2,3,1:T(8,128)S(1)}, f32[64,4,10,1]{0,2,3,1:T(8,128)S(1)}, u32[]{:S(2)}, u32[]{:S(2)}) collective-permute-start(f32[64,4,10,1]{0,2,3,1:T(8,128)S(1)} %copy.16), channel_id=1, source_target_pairs={{2,0},{4,2},{6,4},{8,6},{10,8},{12,10},{14,12},{16,14},{18,16},{20... | collective-permute-start | bytes 30728 | tf_op jit(solution)/shard_map/ppermute | solution.py:13
  56.2 1.9 collective-permute-start.6
  58.4 1.0 collective-permute-done.6
  59.8 1.6 copy.18
  61.4 2.4 pad_maximum_fusion
  64.6 0.9 copy-done.1
  65.5 0.8 fusion
  66.7 1.3 fusion.23
  68.0 6.0 %collective-permute-start.8 = (f32[64,4,1,128]{3,0,2,1:T(8,128)S(1)}, f32[64,4,1,128]{3,0,2,1:T(8,128)S(1)}, u32[]{:S(2)}, u32[]{:S(2)}) collective-permute-start(f32[64,4,1,128]{3,0,2,1:T(8,128)S(1)} %get-tuple-element.20), channel_id=1, source_target_pairs={{0,16},{2,18},{4,20},{6,22},{8,24},{10,26},{12,28},{14,30},{16,32}... | collective-permute-start | bytes 393224 | tf_op jit(solution)/shard_map/ppermute | solution.py:13
  74.1 1.3 collective-permute-start.9
  76.0 5.3 %collective-permute-done.9 = f32[64,4,1,128]{3,0,2,1:T(8,128)S(1)} collective-permute-done((f32[64,4,1,128]{3,0,2,1:T(8,128)S(1)}, f32[64,4,1,128]{3,0,2,1:T(8,128)S(1)}, u32[]{:S(2)}, u32[]{:S(2)}) %collective-permute-start.9) | collective-permute-done | bytes 131104 | tf_op jit(solution)/shard_map/ppermute | solution.py:13
  81.4 1.5 fusion.27
  82.9 2.0 copy.21
  84.9 5.5 %collective-permute-start.10 = (f32[64,4,10,1]{0,2,3,1:T(8,128)S(1)}, f32[64,4,10,1]{0,2,3,1:T(8,128)S(1)}, u32[]{:S(2)}, u32[]{:S(2)}) collective-permute-start(f32[64,4,10,1]{0,2,3,1:T(8,128)S(1)} %copy.21), channel_id=1, source_target_pairs={{0,2},{2,4},{4,6},{6,8},{8,10},{10,12},{12,14},{14,16},{16,18},{18... | collective-permute-start | bytes 30728 | tf_op jit(solution)/shard_map/ppermute | solution.py:13
  91.1 5.1 %collective-permute-start.11 = (f32[64,4,10,1]{0,2,3,1:T(8,128)S(1)}, f32[64,4,10,1]{0,2,3,1:T(8,128)S(1)}, u32[]{:S(2)}, u32[]{:S(2)}) collective-permute-start(f32[64,4,10,1]{0,2,3,1:T(8,128)S(1)} %copy.22), channel_id=1, source_target_pairs={{2,0},{4,2},{6,4},{8,6},{10,8},{12,10},{14,12},{16,14},{18,16},{20... | collective-permute-start | bytes 30728 | tf_op jit(solution)/shard_map/ppermute | solution.py:13
  96.9 1.6 copy.24
  98.4 2.4 pad_maximum_fusion.1
  101.6 0.9 copy-done.2
  103.3 1.3 fusion.20
  104.7 4.5 %collective-permute-start.12 = (f32[64,4,1,128]{3,0,2,1:T(8,128)S(1)}, f32[64,4,1,128]{3,0,2,1:T(8,128)S(1)}, u32[]{:S(2)}, u32[]{:S(2)}) collective-permute-start(f32[64,4,1,128]{3,0,2,1:T(8,128)S(1)} %get-tuple-element.18), channel_id=1, source_target_pairs={{0,16},{2,18},{4,20},{6,22},{8,24},{10,26},{12,28},{14,30},{16,32}... | collective-permute-start | bytes 393224 | tf_op jit(solution)/shard_map/ppermute | solution.py:13
  109.2 1.3 collective-permute-start.13
  111.1 5.3 %collective-permute-done.13 = f32[64,4,1,128]{3,0,2,1:T(8,128)S(1)} collective-permute-done((f32[64,4,1,128]{3,0,2,1:T(8,128)S(1)}, f32[64,4,1,128]{3,0,2,1:T(8,128)S(1)}, u32[]{:S(2)}, u32[]{:S(2)}) %collective-permute-start.13) | collective-permute-done | bytes 131104 | tf_op jit(solution)/shard_map/ppermute | solution.py:13
  116.5 1.5 fusion.26
  118.0 2.0 copy.27
  120.0 1.9 collective-permute-start.14
  122.6 8.8 %collective-permute-start.15 = (f32[64,4,10,1]{0,2,3,1:T(8,128)S(1)}, f32[64,4,10,1]{0,2,3,1:T(8,128)S(1)}, u32[]{:S(2)}, u32[]{:S(2)}) collective-permute-start(f32[64,4,10,1]{0,2,3,1:T(8,128)S(1)} %copy.28), channel_id=1, source_target_pairs={{2,0},{4,2},{6,4},{8,6},{10,8},{12,10},{14,12},{16,14},{18,16},{20... | collective-permute-start | bytes 30728 | tf_op jit(solution)/shard_map/ppermute | solution.py:13
  132.3 1.6 copy.30
  133.8 2.4 pad_maximum_fusion.2
  137.1 0.9 copy-done.3
  138.8 1.3 fusion.17
  140.1 6.4 %collective-permute-start.16 = (f32[64,4,1,128]{3,0,2,1:T(8,128)S(1)}, f32[64,4,1,128]{3,0,2,1:T(8,128)S(1)}, u32[]{:S(2)}, u32[]{:S(2)}) collective-permute-start(f32[64,4,1,128]{3,0,2,1:T(8,128)S(1)} %get-tuple-element.16), channel_id=1, source_target_pairs={{0,16},{2,18},{4,20},{6,22},{8,24},{10,26},{12,28},{14,30},{16,32}... | collective-permute-start | bytes 393224 | tf_op jit(solution)/shard_map/ppermute | solution.py:13
  146.5 1.3 collective-permute-start.17
  148.4 5.3 %collective-permute-done.17 = f32[64,4,1,128]{3,0,2,1:T(8,128)S(1)} collective-permute-done((f32[64,4,1,128]{3,0,2,1:T(8,128)S(1)}, f32[64,4,1,128]{3,0,2,1:T(8,128)S(1)}, u32[]{:S(2)}, u32[]{:S(2)}) %collective-permute-start.17) | collective-permute-done | bytes 131104 | tf_op jit(solution)/shard_map/ppermute | solution.py:13
  153.8 1.5 fusion.25
  155.3 2.0 copy.33
  157.3 1.9 collective-permute-start.18
  159.9 9.0 %collective-permute-start.19 = (f32[64,4,10,1]{0,2,3,1:T(8,128)S(1)}, f32[64,4,10,1]{0,2,3,1:T(8,128)S(1)}, u32[]{:S(2)}, u32[]{:S(2)}) collective-permute-start(f32[64,4,10,1]{0,2,3,1:T(8,128)S(1)} %copy.34), channel_id=1, source_target_pairs={{2,0},{4,2},{6,4},{8,6},{10,8},{12,10},{14,12},{16,14},{18,16},{20... | collective-permute-start | bytes 30728 | tf_op jit(solution)/shard_map/ppermute | solution.py:13
  169.6 1.6 copy.36
  171.1 2.4 pad_maximum_fusion.3
  174.3 0.9 copy-done
  176.0 1.3 fusion.14
  178.0 15.8 %all_to_all.15 = f32[64,4,8,128]{3,2,0,1:T(8,128)S(1)} all-to-all(f32[64,4,8,128]{3,2,0,1:T(8,128)S(1)} %copy.39), channel_id=1, replica_groups=mesh['tiles'=64,'vec'=2] {'vec'}, dimensions={1} | all-to-all | bytes 2097152 | tf_op jit(solution)/shard_map/all_to_all | solution.py:80
  193.8 1.1 copy.52
  194.9 1.4 reshape.96
  196.3 1.1 mul.184
  197.5 2.9 convolution_multiply_fusion
  200.3 1.6 copy.43
  201.9 139.6 %all-reduce.10.cloned.1.call-done = f32[128,128]{0,1:T(8,128)} async-done(((f32[128,128]{0,1:T(8,128)}), f32[128,128]{0,1:T(8,128)}) %all-reduce.10.cloned.1.call-update) | async-done | bytes 65552 | tf_op jit(solution)/shard_map/psum | solution.py:95
  341.5 0.9 copy.42
  342.4 0.9 fusion.24
  343.3 11.7 %cholesky.18 = f32[128,128]{1,0:T(8,128)S(1)} custom-call(f32[128,128]{1,0:T(8,128)S(1)} %fusion.24), custom_call_target="Cholesky" | custom-call | tf_op jit(solution)/shard_map/jit(cholesky)/cholesky | solution.py:96
  (80 shorter events, 19.2 us)
Async XLA Ops:
  7.2 334.3 %all-reduce.10.cloned.1.call-start = ((), (), s32[]{:S(2)}) async-start(), calls=%async_computation.1 | async-start | bytes 131072 | tf_op jit(solution)/shard_map/psum | solution.py:95
  14.1 9.5 %collective-permute-start = (f32[4,4,1,128]{3,2,1,0:T(1,128)S(1)}, f32[4,4,1,128]{3,2,1,0:T(1,128)S(1)}, u32[]{:S(2)}, u32[]{:S(2)}) collective-permute-start(f32[4,4,1,128]{3,2,1,0:T(1,128)S(1)} %get-tuple-element.29), channel_id=1, source_target_pairs={{0,16},{2,18},{4,20},{6,22},{8,24},{10,26},{12,28},{14,30},{16,32}... | collective-permute-start | bytes 24584 | tf_op jit(solution)/shard_map/ppermute | solution.py:13
  20.4 5.9 %collective-permute-start.1 = (f32[4,4,1,128]{3,2,1,0:T(1,128)S(1)}, f32[4,4,1,128]{3,2,1,0:T(1,128)S(1)}, u32[]{:S(2)}, u32[]{:S(2)}) collective-permute-start(f32[4,4,1,128]{3,2,1,0:T(1,128)S(1)} %get-tuple-element.30), channel_id=1, source_target_pairs={{16,0},{18,2},{20,4},{22,6},{24,8},{26,10},{28,12},{30,14},{32,16}... | collective-permute-start | bytes 24584 | tf_op jit(solution)/shard_map/ppermute | solution.py:13
  26.4 11.6 %collective-permute-start.2 = (f32[4,4,10,1]{3,2,1,0:T(8,128)S(1)}, f32[4,4,10,1]{3,2,1,0:T(8,128)S(1)}, u32[]{:S(2)}, u32[]{:S(2)}) collective-permute-start(f32[4,4,10,1]{3,2,1,0:T(8,128)S(1)} %get-tuple-element.27), channel_id=1, source_target_pairs={{0,2},{2,4},{4,6},{6,8},{8,10},{10,12},{12,14},{14,16},{16,18},{18... | collective-permute-start | bytes 1928 | tf_op jit(solution)/shard_map/ppermute | solution.py:13
  31.6 6.5 %collective-permute-start.3 = (f32[4,4,10,1]{3,2,1,0:T(8,128)S(1)}, f32[4,4,10,1]{3,2,1,0:T(8,128)S(1)}, u32[]{:S(2)}, u32[]{:S(2)}) collective-permute-start(f32[4,4,10,1]{3,2,1,0:T(8,128)S(1)} %get-tuple-element.28), channel_id=1, source_target_pairs={{2,0},{4,2},{6,4},{8,6},{10,8},{12,10},{14,12},{16,14},{18,16},{20... | collective-permute-start | bytes 1928 | tf_op jit(solution)/shard_map/ppermute | solution.py:13
  33.5 5.1 %collective-permute-start.4 = (f32[64,4,1,128]{3,0,2,1:T(8,128)S(1)}, f32[64,4,1,128]{3,0,2,1:T(8,128)S(1)}, u32[]{:S(2)}, u32[]{:S(2)}) collective-permute-start(f32[64,4,1,128]{3,0,2,1:T(8,128)S(1)} %get-tuple-element.22), channel_id=1, source_target_pairs={{0,16},{2,18},{4,20},{6,22},{8,24},{10,26},{12,28},{14,30},{16,32}... | collective-permute-start | bytes 393224 | tf_op jit(solution)/shard_map/ppermute | solution.py:13
  36.7 7.2 %collective-permute-start.5 = (f32[64,4,1,128]{3,0,2,1:T(8,128)S(1)}, f32[64,4,1,128]{3,0,2,1:T(8,128)S(1)}, u32[]{:S(2)}, u32[]{:S(2)}) collective-permute-start(f32[64,4,1,128]{3,0,2,1:T(8,128)S(1)} %get-tuple-element.23), channel_id=1, source_target_pairs={{16,0},{18,2},{20,4},{22,6},{24,8},{26,10},{28,12},{30,14},{32,16}... | collective-permute-start | bytes 393224 | tf_op jit(solution)/shard_map/ppermute | solution.py:13
  48.3 11.5 %collective-permute-start.7 = (f32[64,4,10,1]{0,2,3,1:T(8,128)S(1)}, f32[64,4,10,1]{0,2,3,1:T(8,128)S(1)}, u32[]{:S(2)}, u32[]{:S(2)}) collective-permute-start(f32[64,4,10,1]{0,2,3,1:T(8,128)S(1)} %copy.16), channel_id=1, source_target_pairs={{2,0},{4,2},{6,4},{8,6},{10,8},{12,10},{14,12},{16,14},{18,16},{20... | collective-permute-start | bytes 30728 | tf_op jit(solution)/shard_map/ppermute | solution.py:13
  56.2 3.1 collective-permute-start.6
  58.2 42.7 %copy-start.5 = (f32[3,10,130]{2,1,0:T(8,128)}, f32[3,10,130]{2,1,0:T(8,128)S(1)}, u32[]{:S(2)}) copy-start(f32[3,10,130]{2,1,0:T(8,128)S(1)} %slice_bitcast_fusion.3) | copy-start | bytes 46804
  64.1 1.3 copy-start.1
  65.5 1.2 copy-start.4
  68.0 8.0 %collective-permute-start.8 = (f32[64,4,1,128]{3,0,2,1:T(8,128)S(1)}, f32[64,4,1,128]{3,0,2,1:T(8,128)S(1)}, u32[]{:S(2)}, u32[]{:S(2)}) collective-permute-start(f32[64,4,1,128]{3,0,2,1:T(8,128)S(1)} %get-tuple-element.20), channel_id=1, source_target_pairs={{0,16},{2,18},{4,20},{6,22},{8,24},{10,26},{12,28},{14,30},{16,32}... | collective-permute-start | bytes 393224 | tf_op jit(solution)/shard_map/ppermute | solution.py:13
  74.1 7.2 %collective-permute-start.9 = (f32[64,4,1,128]{3,0,2,1:T(8,128)S(1)}, f32[64,4,1,128]{3,0,2,1:T(8,128)S(1)}, u32[]{:S(2)}, u32[]{:S(2)}) collective-permute-start(f32[64,4,1,128]{3,0,2,1:T(8,128)S(1)} %get-tuple-element.21), channel_id=1, source_target_pairs={{16,0},{18,2},{20,4},{22,6},{24,8},{26,10},{28,12},{30,14},{32,16}... | collective-permute-start | bytes 393224 | tf_op jit(solution)/shard_map/ppermute | solution.py:13
  84.9 11.3 %collective-permute-start.10 = (f32[64,4,10,1]{0,2,3,1:T(8,128)S(1)}, f32[64,4,10,1]{0,2,3,1:T(8,128)S(1)}, u32[]{:S(2)}, u32[]{:S(2)}) collective-permute-start(f32[64,4,10,1]{0,2,3,1:T(8,128)S(1)} %copy.21), channel_id=1, source_target_pairs={{0,2},{2,4},{4,6},{6,8},{8,10},{10,12},{12,14},{14,16},{16,18},{18... | collective-permute-start | bytes 30728 | tf_op jit(solution)/shard_map/ppermute | solution.py:13
  91.1 5.8 %collective-permute-start.11 = (f32[64,4,10,1]{0,2,3,1:T(8,128)S(1)}, f32[64,4,10,1]{0,2,3,1:T(8,128)S(1)}, u32[]{:S(2)}, u32[]{:S(2)}) collective-permute-start(f32[64,4,10,1]{0,2,3,1:T(8,128)S(1)} %copy.22), channel_id=1, source_target_pairs={{2,0},{4,2},{6,4},{8,6},{10,8},{12,10},{14,12},{16,14},{18,16},{20... | collective-permute-start | bytes 30728 | tf_op jit(solution)/shard_map/ppermute | solution.py:13
  101.2 1.3 copy-start.2
  104.7 6.4 %collective-permute-start.12 = (f32[64,4,1,128]{3,0,2,1:T(8,128)S(1)}, f32[64,4,1,128]{3,0,2,1:T(8,128)S(1)}, u32[]{:S(2)}, u32[]{:S(2)}) collective-permute-start(f32[64,4,1,128]{3,0,2,1:T(8,128)S(1)} %get-tuple-element.18), channel_id=1, source_target_pairs={{0,16},{2,18},{4,20},{6,22},{8,24},{10,26},{12,28},{14,30},{16,32}... | collective-permute-start | bytes 393224 | tf_op jit(solution)/shard_map/ppermute | solution.py:13
  109.2 7.2 %collective-permute-start.13 = (f32[64,4,1,128]{3,0,2,1:T(8,128)S(1)}, f32[64,4,1,128]{3,0,2,1:T(8,128)S(1)}, u32[]{:S(2)}, u32[]{:S(2)}) collective-permute-start(f32[64,4,1,128]{3,0,2,1:T(8,128)S(1)} %get-tuple-element.19), channel_id=1, source_target_pairs={{16,0},{18,2},{20,4},{22,6},{24,8},{26,10},{28,12},{30,14},{32,16}... | collective-permute-start | bytes 393224 | tf_op jit(solution)/shard_map/ppermute | solution.py:13
  120.0 11.4 %collective-permute-start.14 = (f32[64,4,10,1]{0,2,3,1:T(8,128)S(1)}, f32[64,4,10,1]{0,2,3,1:T(8,128)S(1)}, u32[]{:S(2)}, u32[]{:S(2)}) collective-permute-start(f32[64,4,10,1]{0,2,3,1:T(8,128)S(1)} %copy.27), channel_id=1, source_target_pairs={{0,2},{2,4},{4,6},{6,8},{8,10},{10,12},{12,14},{14,16},{16,18},{18... | collective-permute-start | bytes 30728 | tf_op jit(solution)/shard_map/ppermute | solution.py:13
  122.6 9.6 %collective-permute-start.15 = (f32[64,4,10,1]{0,2,3,1:T(8,128)S(1)}, f32[64,4,10,1]{0,2,3,1:T(8,128)S(1)}, u32[]{:S(2)}, u32[]{:S(2)}) collective-permute-start(f32[64,4,10,1]{0,2,3,1:T(8,128)S(1)} %copy.28), channel_id=1, source_target_pairs={{2,0},{4,2},{6,4},{8,6},{10,8},{12,10},{14,12},{16,14},{18,16},{20... | collective-permute-start | bytes 30728 | tf_op jit(solution)/shard_map/ppermute | solution.py:13
  133.8 2.4 copy-start.6
  136.6 1.3 copy-start.3
  140.1 8.3 %collective-permute-start.16 = (f32[64,4,1,128]{3,0,2,1:T(8,128)S(1)}, f32[64,4,1,128]{3,0,2,1:T(8,128)S(1)}, u32[]{:S(2)}, u32[]{:S(2)}) collective-permute-start(f32[64,4,1,128]{3,0,2,1:T(8,128)S(1)} %get-tuple-element.16), channel_id=1, source_target_pairs={{0,16},{2,18},{4,20},{6,22},{8,24},{10,26},{12,28},{14,30},{16,32}... | collective-permute-start | bytes 393224 | tf_op jit(solution)/shard_map/ppermute | solution.py:13
  146.5 7.2 %collective-permute-start.17 = (f32[64,4,1,128]{3,0,2,1:T(8,128)S(1)}, f32[64,4,1,128]{3,0,2,1:T(8,128)S(1)}, u32[]{:S(2)}, u32[]{:S(2)}) collective-permute-start(f32[64,4,1,128]{3,0,2,1:T(8,128)S(1)} %get-tuple-element.17), channel_id=1, source_target_pairs={{16,0},{18,2},{20,4},{22,6},{24,8},{26,10},{28,12},{30,14},{32,16}... | collective-permute-start | bytes 393224 | tf_op jit(solution)/shard_map/ppermute | solution.py:13
  157.3 11.7 %collective-permute-start.18 = (f32[64,4,10,1]{0,2,3,1:T(8,128)S(1)}, f32[64,4,10,1]{0,2,3,1:T(8,128)S(1)}, u32[]{:S(2)}, u32[]{:S(2)}) collective-permute-start(f32[64,4,10,1]{0,2,3,1:T(8,128)S(1)} %copy.33), channel_id=1, source_target_pairs={{0,2},{2,4},{4,6},{6,8},{8,10},{10,12},{12,14},{14,16},{16,18},{18... | collective-permute-start | bytes 30728 | tf_op jit(solution)/shard_map/ppermute | solution.py:13
  159.9 9.6 %collective-permute-start.19 = (f32[64,4,10,1]{0,2,3,1:T(8,128)S(1)}, f32[64,4,10,1]{0,2,3,1:T(8,128)S(1)}, u32[]{:S(2)}, u32[]{:S(2)}) collective-permute-start(f32[64,4,10,1]{0,2,3,1:T(8,128)S(1)} %copy.34), channel_id=1, source_target_pairs={{2,0},{4,2},{6,4},{8,6},{10,8},{12,10},{14,12},{16,14},{18,16},{20... | collective-permute-start | bytes 30728 | tf_op jit(solution)/shard_map/ppermute | solution.py:13
  171.1 2.4 copy-start.7
  173.9 1.3 copy-start
  178.0 16.9 %copy-start.8 = (f32[8,128]{1,0:T(8,128)S(1)}, f32[8,128]{1,0:T(8,128)}, u32[]{:S(2)}) copy-start(f32[8,128]{1,0:T(8,128)} %param.8) | copy-start | bytes 12292
Sparse Core Ops, SparseCore 0:
  200.5 140.9 all-reduce.9
where the time goes:
time: 365 us; the launch traced here: 364 us
  waiting for transfers between devices  167 us (46%)
  starting transfers between devices  82.1 us (22%)
  other arithmetic  40.4 us (11%)
  local copies, waits for them, and re-layouts  38.2 us (10%)
  between operations  17.2 us (5%)
  blocking collectives  15.8 us (4%)
    psum x1, waiting for transfers between devices, shards(): gram = lax.psum(gram_local, ('tiles', 'vec'))  140 us
    ppermute x20, starting transfers between devices, shifted(): lax.ppermute(value, axis, [(source, source + steps) for source in range(f...  82 us
    ppermute x20, waiting for transfers between devices, shifted(): lax.ppermute(value, axis, [(source, source + steps) for source in range(f...  27.8 us
    all_to_all x1, blocking collectives, shards(): lax.all_to_all(field, 'vec', split_axis=1, concat_axis=0, tiled=True)  15.8 us
    slice x9, local copies, waits for them, and re-layouts, extend(): left_rim = neighbour(stacked[:, :, :, -margin:], 1)  14.2 us
    another operation x3, other arithmetic, shards(): r_factor = jnp.linalg.cholesky(gram).T  12.4 us
    concatenate x5, other arithmetic, extend(): return jnp.concatenate([left_rim, stacked, right_rim], axis=3)  9.82 us
    ppermute x8, local copies, waits for them, and re-layouts, shifted(): lax.ppermute(value, axis, [(source, source + steps) for source in range(f...  8.08 us
  transfers between devices with their start and end apart: 21, of which 14 were waited for; matrix products, arithmetic and copies ran while one was open for 2% of the time, Pallas kernels for 0%

commit v1 on v0

--- a/solution.py
+++ b/solution.py
@@ -5,6 +5,12 @@
 
 TGY = 8
 ITERS = 4
+
+
+def summed_here(block, mesh_axis):
+    terms = lax.all_gather(block, mesh_axis, axis=0, tiled=False)
+    summed = terms.sum(axis=0)
+    return summed
 
 
 def shifted(value, axis, steps):
@@ -92,7 +98,7 @@
         )
         / total_cells
     )
-    gram = lax.psum(gram_local, ("tiles", "vec"))
+    gram = summed_here(gram_local, ("tiles", "vec"))
     r_factor = jnp.linalg.cholesky(gram).T
     return (field, r_factor)
 

time: 365 us -> 538 us (1.47)
  waiting for transfers between devices: 167 us -> 337 us
    all_gather x0 -> x1, waiting for transfers between devices: none -> 310 us  [summed_here(): terms = lax.all_gather(block, mesh_axis, axis=0, tiled=False)]
    psum x1 -> x0, waiting for transfers between devices: 140 us -> none  [shards(): gram = lax.psum(gram_local, ('tiles', 'vec'))]
  transfers between devices with their start and end apart: 21 -> 21, of which waited for: 14 -> 14; matrix products, arithmetic and copies ran while one was open for 2% -> 1% of each run, Pallas kernels for 0% -> 0%
where the time goes in v1:
time: 538 us; the launch traced here: 536 us
  waiting for transfers between devices  337 us (63%)
  starting transfers between devices  82.1 us (15%)
  other arithmetic  43.4 us (8%)
  local copies, waits for them, and re-layouts  37.4 us (7%)
  between operations  17.2 us (3%)
  blocking collectives  15.8 us (3%)
    all_gather x1, waiting for transfers between devices, summed_here(): terms = lax.all_gather(block, mesh_axis, axis=0, tiled=False)  310 us
    ppermute x20, starting transfers between devices, shifted(): lax.ppermute(value, axis, [(source, source + steps) for source in range(f...  82 us
    ppermute x20, waiting for transfers between devices, shifted(): lax.ppermute(value, axis, [(source, source + steps) for source in range(f...  27.8 us
    all_to_all x1, blocking collectives, shards(): lax.all_to_all(field, 'vec', split_axis=1, concat_axis=0, tiled=True)  15.8 us
    slice x9, local copies, waits for them, and re-layouts, extend(): left_rim = neighbour(stacked[:, :, :, -margin:], 1)  14.2 us
    another operation x3, other arithmetic, shards(): r_factor = jnp.linalg.cholesky(gram).T  12.4 us
  transfers between devices with their start and end apart: 21, of which 14 were waited for; matrix products, arithmetic and copies ran while one was open for 1% of the time, Pallas kernels for 0%

profile of v1, /device:TPU:1, one launch (start us, length us, event | category | flops | bytes accessed | tf_op | source)
XLA Modules:
  0.0 536.1 jit_solution(869747838537616942)
XLA Ops:
  7.2 1.5 fusion.34
  13.2 0.8 slice_multiply_fusion.2
  14.1 6.3 %collective-permute-start = (f32[4,4,1,128]{3,2,1,0:T(1,128)S(1)}, f32[4,4,1,128]{3,2,1,0:T(1,128)S(1)}, u32[]{:S(2)}, u32[]{:S(2)}) collective-permute-start(f32[4,4,1,128]{3,2,1,0:T(1,128)S(1)} %get-tuple-element.29), channel_id=1, source_target_pairs={{0,16},{2,18},{4,20},{6,22},{8,24},{10,26},{12,28},{14,30},{16,32}... | collective-permute-start | bytes 24584 | tf_op jit(solution)/shard_map/ppermute | solution.py:19
  20.4 1.3 collective-permute-start.1
  21.7 1.8 copy_multiply_fusion
  23.6 2.7 collective-permute-done.1
  26.4 5.1 collective-permute-start.2
  31.6 1.9 collective-permute-start.3
  33.5 3.2 collective-permute-start.4
  36.7 1.3 collective-permute-start.5
  38.6 5.3 collective-permute-done.5
  44.0 1.5 fusion.28
  45.6 2.0 copy.13
  48.3 8.0 %collective-permute-start.7 = (f32[64,4,10,1]{0,2,3,1:T(8,128)S(1)}, f32[64,4,10,1]{0,2,3,1:T(8,128)S(1)}, u32[]{:S(2)}, u32[]{:S(2)}) collective-permute-start(f32[64,4,10,1]{0,2,3,1:T(8,128)S(1)} %copy.14), channel_id=1, source_target_pairs={{2,0},{4,2},{6,4},{8,6},{10,8},{12,10},{14,12},{16,14},{18,16},{20... | collective-permute-start | bytes 30728 | tf_op jit(solution)/shard_map/ppermute | solution.py:19
  56.2 1.9 collective-permute-start.6
  58.4 1.0 collective-permute-done.6
  59.8 1.6 copy.16
  61.4 2.4 pad_maximum_fusion
  64.6 0.9 copy-done.1
  65.5 0.8 fusion
  66.7 1.3 fusion.23
  68.0 6.0 %collective-permute-start.8 = (f32[64,4,1,128]{3,0,2,1:T(8,128)S(1)}, f32[64,4,1,128]{3,0,2,1:T(8,128)S(1)}, u32[]{:S(2)}, u32[]{:S(2)}) collective-permute-start(f32[64,4,1,128]{3,0,2,1:T(8,128)S(1)} %get-tuple-element.20), channel_id=1, source_target_pairs={{0,16},{2,18},{4,20},{6,22},{8,24},{10,26},{12,28},{14,30},{16,32}... | collective-permute-start | bytes 393224 | tf_op jit(solution)/shard_map/ppermute | solution.py:19
  74.1 1.3 collective-permute-start.9
  76.0 5.3 collective-permute-done.9
  81.4 1.5 fusion.27
  82.9 2.0 copy.19
  84.9 5.5 %collective-permute-start.10 = (f32[64,4,10,1]{0,2,3,1:T(8,128)S(1)}, f32[64,4,10,1]{0,2,3,1:T(8,128)S(1)}, u32[]{:S(2)}, u32[]{:S(2)}) collective-permute-start(f32[64,4,10,1]{0,2,3,1:T(8,128)S(1)} %copy.19), channel_id=1, source_target_pairs={{0,2},{2,4},{4,6},{6,8},{8,10},{10,12},{12,14},{14,16},{16,18},{18... | collective-permute-start | bytes 30728 | tf_op jit(solution)/shard_map/ppermute | solution.py:19
  91.1 5.1 collective-permute-start.11
  96.9 1.6 copy.22
  98.4 2.4 pad_maximum_fusion.1
  101.6 0.9 copy-done.2
  103.3 1.3 fusion.20
  104.7 4.5 collective-permute-start.12
  109.2 1.3 collective-permute-start.13
  111.1 5.3 collective-permute-done.13
  116.5 1.5 fusion.26
  118.0 2.0 copy.25
  120.0 1.9 collective-permute-start.14
  122.6 8.8 %collective-permute-start.15 = (f32[64,4,10,1]{0,2,3,1:T(8,128)S(1)}, f32[64,4,10,1]{0,2,3,1:T(8,128)S(1)}, u32[]{:S(2)}, u32[]{:S(2)}) collective-permute-start(f32[64,4,10,1]{0,2,3,1:T(8,128)S(1)} %copy.26), channel_id=1, source_target_pairs={{2,0},{4,2},{6,4},{8,6},{10,8},{12,10},{14,12},{16,14},{18,16},{20... | collective-permute-start | bytes 30728 | tf_op jit(solution)/shard_map/ppermute | solution.py:19
  132.3 1.6 copy.28
  133.8 2.4 pad_maximum_fusion.2
  137.1 0.9 copy-done.3
  137.9 0.8 fusion.2
  138.8 1.3 fusion.17
  140.1 6.4 %collective-permute-start.16 = (f32[64,4,1,128]{3,0,2,1:T(8,128)S(1)}, f32[64,4,1,128]{3,0,2,1:T(8,128)S(1)}, u32[]{:S(2)}, u32[]{:S(2)}) collective-permute-start(f32[64,4,1,128]{3,0,2,1:T(8,128)S(1)} %get-tuple-element.16), channel_id=1, source_target_pairs={{0,16},{2,18},{4,20},{6,22},{8,24},{10,26},{12,28},{14,30},{16,32}... | collective-permute-start | bytes 393224 | tf_op jit(solution)/shard_map/ppermute | solution.py:19
  146.5 1.3 collective-permute-start.17
  148.4 5.3 collective-permute-done.17
  153.8 1.5 fusion.25
  155.3 2.0 copy.31
  157.3 1.9 collective-permute-start.18
  159.9 9.0 %collective-permute-start.19 = (f32[64,4,10,1]{0,2,3,1:T(8,128)S(1)}, f32[64,4,10,1]{0,2,3,1:T(8,128)S(1)}, u32[]{:S(2)}, u32[]{:S(2)}) collective-permute-start(f32[64,4,10,1]{0,2,3,1:T(8,128)S(1)} %copy.32), channel_id=1, source_target_pairs={{2,0},{4,2},{6,4},{8,6},{10,8},{12,10},{14,12},{16,14},{18,16},{20... | collective-permute-start | bytes 30728 | tf_op jit(solution)/shard_map/ppermute | solution.py:19
  169.6 1.6 copy.34
  171.1 2.4 pad_maximum_fusion.3
  174.3 0.9 copy-done
  176.0 1.3 fusion.14
  178.0 15.8 %all_to_all.15 = f32[64,4,8,128]{3,2,0,1:T(8,128)S(1)} all-to-all(f32[64,4,8,128]{3,2,0,1:T(8,128)S(1)} %copy.37), channel_id=1, replica_groups=mesh['tiles'=64,'vec'=2] {'vec'}, dimensions={1} | all-to-all | bytes 2097152 | tf_op jit(solution)/shard_map/all_to_all | solution.py:86
  193.8 1.1 copy.48
  194.9 1.4 reshape.96
  196.3 1.1 mul.184
  197.5 2.9 convolution_multiply_fusion
  200.3 1.6 copy.40
  201.9 309.6 %all-gather.3.cloned.1.call-done = f32[16384,128]{1,0:T(8,128)} async-done(((f32[128,128]{1,0:T(8,128)}), f32[16384,128]{1,0:T(8,128)}) %all-gather.3.cloned.1.call-update) | async-done | bytes 8388624 | tf_op jit(solution)/shard_map/all_gather | solution.py:11
  511.5 3.8 reduce_sum.9
  515.5 11.7 %cholesky.18 = f32[128,128]{1,0:T(8,128)S(1)} custom-call(f32[128,128]{1,0:T(8,128)S(1)} %fusion.24), custom_call_target="Cholesky" | custom-call | tf_op jit(solution)/shard_map/jit(cholesky)/cholesky | solution.py:102
  (81 shorter events, 18.5 us)
Async XLA Ops:
  7.2 504.4 %all-gather.3.cloned.1.call-start = ((), (), s32[]{:S(2)}) async-start(), calls=%async_computation.1 | async-start | bytes 8454144 | tf_op jit(solution)/shard_map/all_gather | solution.py:11
  14.1 9.5 %collective-permute-start = (f32[4,4,1,128]{3,2,1,0:T(1,128)S(1)}, f32[4,4,1,128]{3,2,1,0:T(1,128)S(1)}, u32[]{:S(2)}, u32[]{:S(2)}) collective-permute-start(f32[4,4,1,128]{3,2,1,0:T(1,128)S(1)} %get-tuple-element.29), channel_id=1, source_target_pairs={{0,16},{2,18},{4,20},{6,22},{8,24},{10,26},{12,28},{14,30},{16,32}... | collective-permute-start | bytes 24584 | tf_op jit(solution)/shard_map/ppermute | solution.py:19
  20.4 5.9 %collective-permute-start.1 = (f32[4,4,1,128]{3,2,1,0:T(1,128)S(1)}, f32[4,4,1,128]{3,2,1,0:T(1,128)S(1)}, u32[]{:S(2)}, u32[]{:S(2)}) collective-permute-start(f32[4,4,1,128]{3,2,1,0:T(1,128)S(1)} %get-tuple-element.30), channel_id=1, source_target_pairs={{16,0},{18,2},{20,4},{22,6},{24,8},{26,10},{28,12},{30,14},{32,16}... | collective-permute-start | bytes 24584 | tf_op jit(solution)/shard_map/ppermute | solution.py:19
  26.4 11.6 %collective-permute-start.2 = (f32[4,4,10,1]{3,2,1,0:T(8,128)S(1)}, f32[4,4,10,1]{3,2,1,0:T(8,128)S(1)}, u32[]{:S(2)}, u32[]{:S(2)}) collective-permute-start(f32[4,4,10,1]{3,2,1,0:T(8,128)S(1)} %get-tuple-element.27), channel_id=1, source_target_pairs={{0,2},{2,4},{4,6},{6,8},{8,10},{10,12},{12,14},{14,16},{16,18},{18... | collective-permute-start | bytes 1928 | tf_op jit(solution)/shard_map/ppermute | solution.py:19
  31.6 6.5 %collective-permute-start.3 = (f32[4,4,10,1]{3,2,1,0:T(8,128)S(1)}, f32[4,4,10,1]{3,2,1,0:T(8,128)S(1)}, u32[]{:S(2)}, u32[]{:S(2)}) collective-permute-start(f32[4,4,10,1]{3,2,1,0:T(8,128)S(1)} %get-tuple-element.28), channel_id=1, source_target_pairs={{2,0},{4,2},{6,4},{8,6},{10,8},{12,10},{14,12},{16,14},{18,16},{20... | collective-permute-start | bytes 1928 | tf_op jit(solution)/shard_map/ppermute | solution.py:19
  33.5 5.1 collective-permute-start.4
  36.7 7.2 %collective-permute-start.5 = (f32[64,4,1,128]{3,0,2,1:T(8,128)S(1)}, f32[64,4,1,128]{3,0,2,1:T(8,128)S(1)}, u32[]{:S(2)}, u32[]{:S(2)}) collective-permute-start(f32[64,4,1,128]{3,0,2,1:T(8,128)S(1)} %get-tuple-element.23), channel_id=1, source_target_pairs={{16,0},{18,2},{20,4},{22,6},{24,8},{26,10},{28,12},{30,14},{32,16}... | collective-permute-start | bytes 393224 | tf_op jit(solution)/shard_map/ppermute | solution.py:19
  48.3 11.5 %collective-permute-start.7 = (f32[64,4,10,1]{0,2,3,1:T(8,128)S(1)}, f32[64,4,10,1]{0,2,3,1:T(8,128)S(1)}, u32[]{:S(2)}, u32[]{:S(2)}) collective-permute-start(f32[64,4,10,1]{0,2,3,1:T(8,128)S(1)} %copy.14), channel_id=1, source_target_pairs={{2,0},{4,2},{6,4},{8,6},{10,8},{12,10},{14,12},{16,14},{18,16},{20... | collective-permute-start | bytes 30728 | tf_op jit(solution)/shard_map/ppermute | solution.py:19
  56.2 3.1 collective-permute-start.6
  58.2 42.7 %copy-start.5 = (f32[3,10,130]{2,1,0:T(8,128)}, f32[3,10,130]{2,1,0:T(8,128)S(1)}, u32[]{:S(2)}) copy-start(f32[3,10,130]{2,1,0:T(8,128)S(1)} %slice_bitcast_fusion.3) | copy-start | bytes 46804
  64.1 1.3 copy-start.1
  65.5 1.2 copy-start.4
  68.0 8.0 %collective-permute-start.8 = (f32[64,4,1,128]{3,0,2,1:T(8,128)S(1)}, f32[64,4,1,128]{3,0,2,1:T(8,128)S(1)}, u32[]{:S(2)}, u32[]{:S(2)}) collective-permute-start(f32[64,4,1,128]{3,0,2,1:T(8,128)S(1)} %get-tuple-element.20), channel_id=1, source_target_pairs={{0,16},{2,18},{4,20},{6,22},{8,24},{10,26},{12,28},{14,30},{16,32}... | collective-permute-start | bytes 393224 | tf_op jit(solution)/shard_map/ppermute | solution.py:19
  74.1 7.2 %collective-permute-start.9 = (f32[64,4,1,128]{3,0,2,1:T(8,128)S(1)}, f32[64,4,1,128]{3,0,2,1:T(8,128)S(1)}, u32[]{:S(2)}, u32[]{:S(2)}) collective-permute-start(f32[64,4,1,128]{3,0,2,1:T(8,128)S(1)} %get-tuple-element.21), channel_id=1, source_target_pairs={{16,0},{18,2},{20,4},{22,6},{24,8},{26,10},{28,12},{30,14},{32,16}... | collective-permute-start | bytes 393224 | tf_op jit(solution)/shard_map/ppermute | solution.py:19
  84.9 11.3 %collective-permute-start.10 = (f32[64,4,10,1]{0,2,3,1:T(8,128)S(1)}, f32[64,4,10,1]{0,2,3,1:T(8,128)S(1)}, u32[]{:S(2)}, u32[]{:S(2)}) collective-permute-start(f32[64,4,10,1]{0,2,3,1:T(8,128)S(1)} %copy.19), channel_id=1, source_target_pairs={{0,2},{2,4},{4,6},{6,8},{8,10},{10,12},{12,14},{14,16},{16,18},{18... | collective-permute-start | bytes 30728 | tf_op jit(solution)/shard_map/ppermute | solution.py:19
  91.1 5.8 %collective-permute-start.11 = (f32[64,4,10,1]{0,2,3,1:T(8,128)S(1)}, f32[64,4,10,1]{0,2,3,1:T(8,128)S(1)}, u32[]{:S(2)}, u32[]{:S(2)}) collective-permute-start(f32[64,4,10,1]{0,2,3,1:T(8,128)S(1)} %copy.20), channel_id=1, source_target_pairs={{2,0},{4,2},{6,4},{8,6},{10,8},{12,10},{14,12},{16,14},{18,16},{20... | collective-permute-start | bytes 30728 | tf_op jit(solution)/shard_map/ppermute | solution.py:19
  101.2 1.3 copy-start.2
  104.7 6.4 %collective-permute-start.12 = (f32[64,4,1,128]{3,0,2,1:T(8,128)S(1)}, f32[64,4,1,128]{3,0,2,1:T(8,128)S(1)}, u32[]{:S(2)}, u32[]{:S(2)}) collective-permute-start(f32[64,4,1,128]{3,0,2,1:T(8,128)S(1)} %get-tuple-element.18), channel_id=1, source_target_pairs={{0,16},{2,18},{4,20},{6,22},{8,24},{10,26},{12,28},{14,30},{16,32}... | collective-permute-start | bytes 393224 | tf_op jit(solution)/shard_map/ppermute | solution.py:19
  109.2 7.2 %collective-permute-start.13 = (f32[64,4,1,128]{3,0,2,1:T(8,128)S(1)}, f32[64,4,1,128]{3,0,2,1:T(8,128)S(1)}, u32[]{:S(2)}, u32[]{:S(2)}) collective-permute-start(f32[64,4,1,128]{3,0,2,1:T(8,128)S(1)} %get-tuple-element.19), channel_id=1, source_target_pairs={{16,0},{18,2},{20,4},{22,6},{24,8},{26,10},{28,12},{30,14},{32,16}... | collective-permute-start | bytes 393224 | tf_op jit(solution)/shard_map/ppermute | solution.py:19
  120.0 11.4 %collective-permute-start.14 = (f32[64,4,10,1]{0,2,3,1:T(8,128)S(1)}, f32[64,4,10,1]{0,2,3,1:T(8,128)S(1)}, u32[]{:S(2)}, u32[]{:S(2)}) collective-permute-start(f32[64,4,10,1]{0,2,3,1:T(8,128)S(1)} %copy.25), channel_id=1, source_target_pairs={{0,2},{2,4},{4,6},{6,8},{8,10},{10,12},{12,14},{14,16},{16,18},{18... | collective-permute-start | bytes 30728 | tf_op jit(solution)/shard_map/ppermute | solution.py:19
  122.6 9.6 %collective-permute-start.15 = (f32[64,4,10,1]{0,2,3,1:T(8,128)S(1)}, f32[64,4,10,1]{0,2,3,1:T(8,128)S(1)}, u32[]{:S(2)}, u32[]{:S(2)}) collective-permute-start(f32[64,4,10,1]{0,2,3,1:T(8,128)S(1)} %copy.26), channel_id=1, source_target_pairs={{2,0},{4,2},{6,4},{8,6},{10,8},{12,10},{14,12},{16,14},{18,16},{20... | collective-permute-start | bytes 30728 | tf_op jit(solution)/shard_map/ppermute | solution.py:19
  133.8 2.4 copy-start.6
  136.6 1.3 copy-start.3
  140.1 8.3 %collective-permute-start.16 = (f32[64,4,1,128]{3,0,2,1:T(8,128)S(1)}, f32[64,4,1,128]{3,0,2,1:T(8,128)S(1)}, u32[]{:S(2)}, u32[]{:S(2)}) collective-permute-start(f32[64,4,1,128]{3,0,2,1:T(8,128)S(1)} %get-tuple-element.16), channel_id=1, source_target_pairs={{0,16},{2,18},{4,20},{6,22},{8,24},{10,26},{12,28},{14,30},{16,32}... | collective-permute-start | bytes 393224 | tf_op jit(solution)/shard_map/ppermute | solution.py:19
  146.5 7.2 %collective-permute-start.17 = (f32[64,4,1,128]{3,0,2,1:T(8,128)S(1)}, f32[64,4,1,128]{3,0,2,1:T(8,128)S(1)}, u32[]{:S(2)}, u32[]{:S(2)}) collective-permute-start(f32[64,4,1,128]{3,0,2,1:T(8,128)S(1)} %get-tuple-element.17), channel_id=1, source_target_pairs={{16,0},{18,2},{20,4},{22,6},{24,8},{26,10},{28,12},{30,14},{32,16}... | collective-permute-start | bytes 393224 | tf_op jit(solution)/shard_map/ppermute | solution.py:19
  157.3 11.7 %collective-permute-start.18 = (f32[64,4,10,1]{0,2,3,1:T(8,128)S(1)}, f32[64,4,10,1]{0,2,3,1:T(8,128)S(1)}, u32[]{:S(2)}, u32[]{:S(2)}) collective-permute-start(f32[64,4,10,1]{0,2,3,1:T(8,128)S(1)} %copy.31), channel_id=1, source_target_pairs={{0,2},{2,4},{4,6},{6,8},{8,10},{10,12},{12,14},{14,16},{16,18},{18... | collective-permute-start | bytes 30728 | tf_op jit(solution)/shard_map/ppermute | solution.py:19
  159.9 9.6 %collective-permute-start.19 = (f32[64,4,10,1]{0,2,3,1:T(8,128)S(1)}, f32[64,4,10,1]{0,2,3,1:T(8,128)S(1)}, u32[]{:S(2)}, u32[]{:S(2)}) collective-permute-start(f32[64,4,10,1]{0,2,3,1:T(8,128)S(1)} %copy.32), channel_id=1, source_target_pairs={{2,0},{4,2},{6,4},{8,6},{10,8},{12,10},{14,12},{16,14},{18,16},{20... | collective-permute-start | bytes 30728 | tf_op jit(solution)/shard_map/ppermute | solution.py:19
  171.1 2.4 copy-start.7
  173.9 1.3 copy-start
  178.0 16.9 %copy-start.8 = (f32[8,128]{1,0:T(8,128)S(1)}, f32[8,128]{1,0:T(8,128)}, u32[]{:S(2)}) copy-start(f32[8,128]{1,0:T(8,128)} %param.8) | copy-start | bytes 12292
Sparse Core Ops, SparseCore 0:
  200.5 311.0 all-gather.2
